TPU v7x, 256 devices: a whole 4x4x8 slice. The times are simulated.
256 devices in a mesh: row: 16 (over y, z_lo, core), col: 16 (over z_hi, x).
Axes of the slice: x: 4, y: 4, z: 8 (z_hi: 4, z_lo: 2; z = z_hi * 2 + z_lo), core: 2. Of those that a mesh axis runs over, the one named last changes fastest.
Arguments:
- pairs: bfloat16 [2, 256, 20480], P(None, None, ('row', 'col')), may hold values from -12 to 12
- prior: bfloat16 [2, 20480, 20480], P(None, 'row', 'col'), may hold values from -0.025146484 to 0.025146484
- val_band: int32 [256], replicated, may hold values from 0 to 255
- cond_band: int32 [256], replicated, may hold values from 0 to 2047
- val_energy: float32 [256], replicated, may hold values from -3 to -1
- cond_energy: float32 [2048], replicated, may hold values from 0.5 to 2.5
- coul_root: float32 [20480], replicated, may hold values from 0.3 to 1.5
- potential: float32 [2, 128, 20480], P(None, 'col', 'row'), may hold values from -6 to 6
Outputs:
- screened: float32 [2, 128, 20480], P(None, 'col', 'row')
All inputs are finite; a program needn't handle non-finite values.
Results may differ from a plain program's by a relative error of at most 0.0007.
Values may be sent and summed in bfloat16 or wider, within the bound.
No kernel may reach another device: no remote copies, remote signals or barrier semaphores. Data moves between devices by JAX's collectives and lax.ppermute only.
A program may use at most 128 MiB of HBM per device.

v0:
```python
import functools

import jax
import jax.numpy as jnp
from jax import lax
from jax.experimental import pallas as pl
from jax.experimental.pallas import tpu as pltpu
from jax.sharding import PartitionSpec as P


NG = 20480
ITERS = 2
FULL = 32000.0
BLOCK = 256
AXES = ("row", "col")


def moves(function):
    pairs = []
    for row in range(16):
        for col in range(16):
            to_row, to_col = function(row, col)
            pairs.append((row * 16 + col, to_row * 16 + to_col))
    return pairs


SWAP = moves(lambda r, c: ((c + 8) % 16, r))
CORE = moves(lambda r, c: (r ^ 1, c))
NEAR_Z = moves(lambda r, c: (r ^ 2, c))
ALONG_Y = [moves(lambda r, c, s=s: ((r + 4 * s) % 16, c)) for s in range(4)]
ALONG_X = [moves(lambda r, c, s=s: (r, (c & ~3) | ((c + s) & 3))) for s in range(4)]
FAR_Z = [moves(lambda r, c, s=s: (r, (c + 4 * s) % 16)) for s in range(4)]
STEPS = (1, 3, 2)


def send(value, pairs):
    return lax.ppermute(value, AXES, pairs)


def pick_energy(band, energy):
    levels = jnp.arange(energy.shape[0], dtype=jnp.int32)
    return jnp.sum(jnp.where(band[:, None] == levels[None, :], energy[None, :], 0.0), axis=1)


def encode(value):
    top = jnp.max(jnp.abs(value), axis=-1, keepdims=True)
    power = jnp.clip(jnp.ceil(jnp.log2(jnp.maximum(top, 1e-30))), -100.0, 125.0)
    scaled = jnp.round(value * (jnp.exp2(-power) * FULL)).astype(jnp.int32).astype(jnp.int16)
    powers = jnp.broadcast_to(power.astype(jnp.int32), value.shape[:-1] + (128,)).astype(jnp.int16)
    return jnp.concatenate([scaled, powers], axis=-1)


def decode(coded):
    power = coded[..., -128:-127].astype(jnp.float32)
    return coded[..., :-128].astype(jnp.float32) * (jnp.exp2(power) * (1.0 / FULL))


def split(value):
    high = lax.reduce_precision(value, 8, 7)
    return high.astype(jnp.bfloat16), (value - high).astype(jnp.bfloat16)


def ring_order(own, pairs, position):
    parts = {0: own, **{step: send(own, pairs[step]) for step in STEPS}}
    ring = jnp.stack([parts[step] for step in range(4)])
    return jnp.stack(
        [lax.dynamic_index_in_dim(ring, (position - at) % 4, 0, keepdims=False) for at in range(4)]
    )


def gather_rows(block):
    pair = jnp.stack([block, send(block, NEAR_Z)])
    parts = {0: pair, **{step: send(pair, ALONG_Y[step]) for step in STEPS}}
    ring = jnp.stack([parts[step] for step in range(4)])
    return ring, send(ring, CORE)


def gather_cols(block, col_index):
    x, z = col_index & 3, col_index >> 2
    column = ring_order(block, FAR_Z, z)
    plane = ring_order(column, ALONG_X, x)
    return jnp.swapaxes(plane, 0, 1).reshape((16,) + block.shape)


def sum_rows(value):
    value = value + send(value, CORE)
    value = value + send(value, NEAR_Z)
    return value + functools.reduce(jnp.add, [send(value, ALONG_Y[step]) for step in STEPS])


def dot(left, right, contract):
    return lax.dot_general(left, right, ((contract[0], contract[1]), ((), ())), preferred_element_type=jnp.float32)


def respond_body(place_ref, own_core_ref, other_core_ref, prior_ref, own_ref, *refs):
    sent, (rows_ref, sum_ref, kept_ref, sems) = refs[:3], refs[3:]
    copies = []
    for at in range(1280 // BLOCK):
        rows = pl.ds(at * BLOCK, BLOCK)
        copies.append(pltpu.make_async_copy(prior_ref.at[:, rows], kept_ref.at[:, rows], sems.at[at]))
        copies[-1].start()
    core, near_z, along_y, x = [place_ref[k] for k in range(4)]
    for k, ref in enumerate((own_core_ref, other_core_ref)):
        for s in range(4):
            for d in range(2):
                coded = ref[s, d]
                power = coded[:, 1280:].astype(jnp.float32)[:, :1]
                value = coded[:, :1280].astype(jnp.float32) * (jnp.exp2(power) * (1.0 / FULL))
                high = value.astype(jnp.bfloat16)
                low = (value - high.astype(jnp.float32)).astype(jnp.bfloat16)
                block = ((along_y - s + 2) & 3) * 4 + ((near_z + d) & 1) * 2 + ((core + k) & 1)
                rows_ref[pl.ds(pl.multiple_of(block * 16, 16), 16), :] = high
                rows_ref[pl.ds(pl.multiple_of(block * 16 + 256, 16), 16), :] = low
    for at in range(0, 1280, BLOCK):
        copies[at // BLOCK].wait()

        def product(part):
            value = dot(rows_ref[...], kept_ref[part, at : at + BLOCK], ((1,), (1,)))
            return (value[:256] + value[256:]).reshape(16, 2, 8, BLOCK)

        by_real, by_imag = product(0), product(1)
        real = by_real[:, 0] - by_imag[:, 1]
        imag = by_imag[:, 0] + by_real[:, 1]
        sum_ref[:, :, 0:8, at : at + BLOCK] = real.reshape(4, 4, 8, BLOCK)
        sum_ref[:, :, 8:16, at : at + BLOCK] = imag.reshape(4, 4, 8, BLOCK)
    for z in range(4):
        own_ref[z] = sum_ref[z, x]
        for step in range(1, 4):
            value = sum_ref[z, (x + step) & 3]
            top = jnp.max(jnp.abs(value), axis=-1, keepdims=True)
            power = jnp.clip(jnp.ceil(jnp.log2(jnp.maximum(top, 1e-30))), -100.0, 125.0)
            scaled = jnp.round(value * (jnp.exp2(-power) * FULL)).astype(jnp.int32)
            sent[step - 1][z, :, :1280] = scaled.astype(jnp.int16)
            powers = jnp.broadcast_to(power.astype(jnp.int32), (16, 128))
            sent[step - 1][z, :, 1280:] = powers.astype(jnp.int16)


def respond(own_core, other_core, prior, place):
    smem, vmem = pl.BlockSpec(memory_space=pltpu.SMEM), pl.BlockSpec(memory_space=pltpu.VMEM)
    return pl.pallas_call(
        respond_body,
        in_specs=[smem, vmem, vmem, pl.BlockSpec(memory_space=pltpu.HBM)],
        out_specs=[vmem] * 4,
        out_shape=[jax.ShapeDtypeStruct((4, 16, 1280), jnp.float32)]
        + [jax.ShapeDtypeStruct((4, 16, 1408), jnp.int16)] * 3,
        scratch_shapes=[
            pltpu.VMEM((512, 1280), jnp.bfloat16),
            pltpu.VMEM((4, 4, 16, 1280), jnp.float32),
            pltpu.VMEM((2, 1280, 1280), jnp.bfloat16),
            pltpu.SemaphoreType.DMA((1280 // BLOCK,)),
        ],
        compiler_params=pltpu.CompilerParams(vmem_limit_bytes=48 << 20),
        cost_estimate=pl.CostEstimate(flops=3400000000, transcendentals=0, bytes_accessed=8000000),
        name="respond",
    )(place, own_core, other_core, prior)


def project(scaled, weighted):
    high, low = split(scaled)
    value = dot(jnp.concatenate([high, low], axis=0), weighted, ((1,), (0,)))
    value = value[:16] + value[16:]
    real, imag = value[:, :256], value[:, 256:]
    return jnp.concatenate([real[:8] - imag[8:], imag[:8] + real[8:]], axis=0)


def pair_part(summed, elements):
    high, low = split(summed)
    rows = jnp.concatenate([high, low], axis=0)
    by_real = dot(rows, elements[:, :256], ((1,), (1,)))
    by_imag = dot(rows, elements[:, 256:], ((1,), (1,)))
    by_real = by_real[:16] + by_real[16:]
    by_imag = by_imag[:16] + by_imag[16:]
    return jnp.concatenate([by_real[:8] + by_imag[8:], by_real[8:] - by_imag[:8]], axis=0)


def reduce_cols(own, sent, z):
    received = [send(sent[step - 1], ALONG_X[step]) for step in STEPS]
    total = own + functools.reduce(jnp.add, [decode(part) for part in received])
    coded = encode(total)
    received = [send(lax.dynamic_index_in_dim(coded, (z + step) % 4, 0, keepdims=False), FAR_Z[step]) for step in STEPS]
    own = lax.dynamic_index_in_dim(total, z, 0, keepdims=False)
    return own + functools.reduce(jnp.add, [decode(part) for part in received])


def local(pairs, prior, val_band, cond_band, val_energy, cond_energy, coul_root, potential):
    row_index = lax.axis_index("row")
    col_index = lax.axis_index("col")
    gain = lax.dynamic_slice_in_dim(coul_root, row_index * 1280, 1280, 0)
    potential = potential.reshape(16, 1280)
    place = jnp.stack([row_index & 1, (row_index >> 1) & 1, row_index >> 2, col_index & 3])
    block = jnp.concatenate([pairs[0].T, pairs[1].T], axis=1)
    iterate = potential
    for step in range(ITERS):
        coded = send(encode(iterate * gain), SWAP)
        if step == 0:
            elements = gather_cols(block, col_index).reshape(1280, 512)
            weights = 1.0 / (pick_energy(cond_band, cond_energy) - pick_energy(val_band, val_energy))
            weights = jnp.concatenate([weights, weights])
            weighted = (weights[None, :] * elements.astype(jnp.float32)).astype(jnp.bfloat16)
        own, *sent = respond(*gather_rows(coded), prior, place)
        reduced = reduce_cols(own, sent, col_index >> 2)
        projected = project(iterate * gain, weighted)
        projected = sum_rows(projected) / NG
        applied = gain * (reduced + pair_part(projected, elements))
        iterate = iterate + 0.5 * (potential - iterate - applied)
    return iterate.reshape(2, 8, 1280)


def solution(mesh):
    in_specs = (
        P(None, None, ("row", "col")),
        P(None, "row", "col"),
        P(),
        P(),
        P(),
        P(),
        P(),
        P(None, "col", "row"),
    )
    return jax.shard_map(local, mesh=mesh, in_specs=in_specs, out_specs=P(None, "col", "row"), check_vma=False)
```

profile of v0, /device:TPU:8, one launch (start us, length us, event | category | flops | bytes accessed | tf_op | source)
XLA Modules:
  0.0 145.1 jit_solution(13682820316941688104)
XLA Ops:
  0.8 6.4 %collective-permute-start.14 = (bf16[80,512]{1,0:T(8,128)(2,1)S(1)}, bf16[80,512]{1,0:T(8,128)(2,1)S(1)}, u32[]{:S(2)}, u32[]{:S(2)}) collective-permute-start(bf16[80,512]{1,0:T(8,128)(2,1)S(1)} %get-tuple-element.62), channel_id=1, source_target_pairs={{0,12},{1,13},{2,14},{3,15},{4,0},{5,1},{6,2},{7,3},{8,4},{9,5},{1... | collective-permute-start | bytes 245768 | tf_op jit(solution)/shard_map/ppermute | solution.py:37
  8.2 2.8 %collective-permute-start.12 = (bf16[80,512]{1,0:T(8,128)(2,1)S(1)}, bf16[80,512]{1,0:T(8,128)(2,1)S(1)}, u32[]{:S(2)}, u32[]{:S(2)}) collective-permute-start(bf16[80,512]{1,0:T(8,128)(2,1)S(1)} %get-tuple-element.62), channel_id=1, source_target_pairs={{0,4},{1,5},{2,6},{3,7},{4,8},{5,9},{6,10},{7,11},{8,12},{9,13},{1... | collective-permute-start | bytes 245768 | tf_op jit(solution)/shard_map/ppermute | solution.py:37
  14.0 3.7 %collective-permute-start = (s16[16,1408]{1,0:T(8,128)(2,1)S(1)}, s16[16,1408]{1,0:T(8,128)(2,1)S(1)}, u32[]{:S(2)}, u32[]{:S(2)}) collective-permute-start(s16[16,1408]{1,0:T(8,128)(2,1)S(1)} %pad_add_fusion.4), channel_id=1, source_target_pairs={{0,128},{1,144},{2,160},{3,176},{4,192},{5,208},{6,224},{7,240},{8... | collective-permute-start | bytes 135176 | tf_op jit(solution)/shard_map/ppermute | solution.py:37
  25.7 4.8 %collective-permute-done.17 = bf16[4,80,512]{2,1,0:T(8,128)(2,1)S(1)} collective-permute-done((bf16[4,80,512]{2,1,0:T(8,128)(2,1)S(1)}, bf16[4,80,512]{2,1,0:T(8,128)(2,1)S(1)}, u32[]{:S(2)}, u32[]{:S(2)}) %collective-permute-start.17) | collective-permute-done | bytes 327712 | tf_op jit(solution)/shard_map/ppermute | solution.py:37
  30.5 3.3 %collective-permute-done.16 = bf16[4,80,512]{2,1,0:T(8,128)(2,1)S(1)} collective-permute-done((bf16[4,80,512]{2,1,0:T(8,128)(2,1)S(1)}, bf16[4,80,512]{2,1,0:T(8,128)(2,1)S(1)}, u32[]{:S(2)}, u32[]{:S(2)}) %collective-permute-start.16) | collective-permute-done | bytes 327712 | tf_op jit(solution)/shard_map/ppermute | solution.py:37
  33.8 6.8 %collective-permute-done.15 = bf16[4,80,512]{2,1,0:T(8,128)(2,1)S(1)} collective-permute-done((bf16[4,80,512]{2,1,0:T(8,128)(2,1)S(1)}, bf16[4,80,512]{2,1,0:T(8,128)(2,1)S(1)}, u32[]{:S(2)}, u32[]{:S(2)}) %collective-permute-start.15) | collective-permute-done | bytes 327712 | tf_op jit(solution)/shard_map/ppermute | solution.py:37
  47.7 3.9 %collective-permute-start.22 = (f32[16,256]{1,0:T(8,128)S(1)}, f32[16,256]{1,0:T(8,128)S(1)}, u32[]{:S(2)}, u32[]{:S(2)}) collective-permute-start(f32[16,256]{1,0:T(8,128)S(1)} %add.246), channel_id=1, source_target_pairs={{0,128},{1,129},{2,130},{3,131},{4,132},{5,133},{6,134},{7,135},{8... | collective-permute-start | bytes 49160 | tf_op jit(solution)/shard_map/ppermute | solution.py:37
  51.6 2.0 %collective-permute-start.21 = (f32[16,256]{1,0:T(8,128)S(1)}, f32[16,256]{1,0:T(8,128)S(1)}, u32[]{:S(2)}, u32[]{:S(2)}) collective-permute-start(f32[16,256]{1,0:T(8,128)S(1)} %add.246), channel_id=1, source_target_pairs={{0,192},{1,193},{2,194},{3,195},{4,196},{5,197},{6,198},{7,199},{8... | collective-permute-start | bytes 49160 | tf_op jit(solution)/shard_map/ppermute | solution.py:37
  56.0 6.7 %respond.2 = (f32[4,16,1280]{2,1,0:T(8,128)S(1)}, s16[4,16,1408]{2,1,0:T(8,128)(2,1)S(1)}, s16[4,16,1408]{2,1,0:T(8,128)(2,1)S(1)}, s16[4,16,1408]{2,1,0:T(8,128)(2,1)S(1)}) custom-call(s32[4]{0:T(128)S(1)} %pad_add_fusion.6.place_ref, s16[4,2,16,1408]{3,2,1,0:T(8,128)(2,1)S(1)} %pad_add_fusion.own_core_ref, ...), custom_call_target="tpu_custom_call" | custom-call | flops 3400000000 | bytes 8000000 | tf_op jit(solution)/shard_map/respond/pallas_call | solution.py:140
  66.2 5.6 %collective-permute-done.8 = s16[4,16,1408]{2,1,0:T(8,128)(2,1)S(1)} collective-permute-done((s16[4,16,1408]{2,1,0:T(8,128)(2,1)S(1)}, s16[4,16,1408]{2,1,0:T(8,128)(2,1)S(1)}, u32[]{:S(2)}, u32[]{:S(2)}) %collective-permute-start.8) | collective-permute-done | bytes 180256 | tf_op jit(solution)/shard_map/ppermute | solution.py:37
  76.7 3.1 %collective-permute-start.10 = (s16[16,1408]{1,0:T(8,128)(2,1)S(1)}, s16[16,1408]{1,0:T(8,128)(2,1)S(1)}, u32[]{:S(2)}, u32[]{:S(2)}) collective-permute-start(s16[16,1408]{1,0:T(8,128)(2,1)S(1)} %get-tuple-element.45), channel_id=1, source_target_pairs={{0,12},{1,13},{2,14},{3,15},{4,0},{5,1},{6,2},{7,3},{8,4},{9,5},{1... | collective-permute-start | bytes 135176 | tf_op jit(solution)/shard_map/ppermute | solution.py:37
  79.8 3.6 %collective-permute-done.11 = s16[16,1408]{1,0:T(8,128)(2,1)S(1)} collective-permute-done((s16[16,1408]{1,0:T(8,128)(2,1)S(1)}, s16[16,1408]{1,0:T(8,128)(2,1)S(1)}, u32[]{:S(2)}, u32[]{:S(2)}) %collective-permute-start.11) | collective-permute-done | bytes 45088 | tf_op jit(solution)/shard_map/ppermute | solution.py:37
  83.7 2.4 %collective-permute-done.9 = s16[16,1408]{1,0:T(8,128)(2,1)S(1)} collective-permute-done((s16[16,1408]{1,0:T(8,128)(2,1)S(1)}, s16[16,1408]{1,0:T(8,128)(2,1)S(1)}, u32[]{:S(2)}, u32[]{:S(2)}) %collective-permute-start.9) | collective-permute-done | bytes 45088 | tf_op jit(solution)/shard_map/ppermute | solution.py:37
  90.0 2.0 %collective-permute-done.36 = f32[16,256]{1,0:T(8,128)S(1)} collective-permute-done((f32[16,256]{1,0:T(8,128)S(1)}, f32[16,256]{1,0:T(8,128)S(1)}, u32[]{:S(2)}, u32[]{:S(2)}) %collective-permute-start.36) | collective-permute-done | bytes 16416 | tf_op jit(solution)/shard_map/ppermute | solution.py:37
  93.8 3.1 %collective-permute-start.37 = (f32[16,256]{1,0:T(8,128)S(1)}, f32[16,256]{1,0:T(8,128)S(1)}, u32[]{:S(2)}, u32[]{:S(2)}) collective-permute-start(f32[16,256]{1,0:T(8,128)S(1)} %add.264), channel_id=1, source_target_pairs={{0,64},{1,65},{2,66},{3,67},{4,68},{5,69},{6,70},{7,71},{8,72},{9,... | collective-permute-start | bytes 49160 | tf_op jit(solution)/shard_map/ppermute | solution.py:37
  96.9 3.0 %collective-permute-start.24 = (s16[16,1408]{1,0:T(8,128)(2,1)S(1)}, s16[16,1408]{1,0:T(8,128)(2,1)S(1)}, u32[]{:S(2)}, u32[]{:S(2)}) collective-permute-start(s16[16,1408]{1,0:T(8,128)(2,1)S(1)} %collective-permute-done.23), channel_id=1, source_target_pairs={{0,32},{1,33},{2,34},{3,35},{4,36},{5,37},{6,38},{7,39},{8,40},{9,... | collective-permute-start | bytes 135176 | tf_op jit(solution)/shard_map/ppermute | solution.py:37
  107.4 2.2 %collective-permute-done.26 = s16[2,16,1408]{2,1,0:T(8,128)(2,1)S(1)} collective-permute-done((s16[2,16,1408]{2,1,0:T(8,128)(2,1)S(1)}, s16[2,16,1408]{2,1,0:T(8,128)(2,1)S(1)}, u32[]{:S(2)}, u32[]{:S(2)}) %collective-permute-start.26) | collective-permute-done | bytes 90144 | tf_op jit(solution)/shard_map/ppermute | solution.py:37
  111.4 6.7 %respond.3 = (f32[4,16,1280]{2,1,0:T(8,128)S(1)}, s16[4,16,1408]{2,1,0:T(8,128)(2,1)S(1)}, s16[4,16,1408]{2,1,0:T(8,128)(2,1)S(1)}, s16[4,16,1408]{2,1,0:T(8,128)(2,1)S(1)}) custom-call(s32[4]{0:T(128)S(1)} %pad_add_fusion.6.place_ref, s16[4,2,16,1408]{3,2,1,0:T(8,128)(2,1)S(1)} %pad_add_fusion.1.own_core_ref, ...), custom_call_target="tpu_custom_call" | custom-call | flops 3400000000 | bytes 8000000 | tf_op jit(solution)/shard_map/respond/pallas_call | solution.py:140
  118.1 3.4 %collective-permute-start.31 = (s16[4,16,1408]{2,1,0:T(8,128)(2,1)S(1)}, s16[4,16,1408]{2,1,0:T(8,128)(2,1)S(1)}, u32[]{:S(2)}, u32[]{:S(2)}) collective-permute-start(s16[4,16,1408]{2,1,0:T(8,128)(2,1)S(1)} %get-tuple-element.20), channel_id=1, source_target_pairs={{0,2},{1,3},{2,0},{3,1},{4,6},{5,7},{6,4},{7,5},{8,10},{9,11},{10,... | collective-permute-start | bytes 540680 | tf_op jit(solution)/shard_map/ppermute | solution.py:37
  123.6 3.5 %collective-permute-done.31 = s16[4,16,1408]{2,1,0:T(8,128)(2,1)S(1)} collective-permute-done((s16[4,16,1408]{2,1,0:T(8,128)(2,1)S(1)}, s16[4,16,1408]{2,1,0:T(8,128)(2,1)S(1)}, u32[]{:S(2)}, u32[]{:S(2)}) %collective-permute-start.31) | collective-permute-done | bytes 180256 | tf_op jit(solution)/shard_map/ppermute | solution.py:37
  127.2 3.4 %collective-permute-done.30 = s16[4,16,1408]{2,1,0:T(8,128)(2,1)S(1)} collective-permute-done((s16[4,16,1408]{2,1,0:T(8,128)(2,1)S(1)}, s16[4,16,1408]{2,1,0:T(8,128)(2,1)S(1)}, u32[]{:S(2)}, u32[]{:S(2)}) %collective-permute-start.30) | collective-permute-done | bytes 180256 | tf_op jit(solution)/shard_map/ppermute | solution.py:37
  131.3 4.0 %collective-permute-start.34 = (s16[16,1408]{1,0:T(8,128)(2,1)S(1)}, s16[16,1408]{1,0:T(8,128)(2,1)S(1)}, u32[]{:S(2)}, u32[]{:S(2)}) collective-permute-start(s16[16,1408]{1,0:T(8,128)(2,1)S(1)} %get-tuple-element.43), channel_id=1, source_target_pairs={{0,8},{1,9},{2,10},{3,11},{4,12},{5,13},{6,14},{7,15},{8,0},{9,1},... | collective-permute-start | bytes 135176 | tf_op jit(solution)/shard_map/ppermute | solution.py:37
  135.3 2.7 %collective-permute-start.33 = (s16[16,1408]{1,0:T(8,128)(2,1)S(1)}, s16[16,1408]{1,0:T(8,128)(2,1)S(1)}, u32[]{:S(2)}, u32[]{:S(2)}) collective-permute-start(s16[16,1408]{1,0:T(8,128)(2,1)S(1)} %get-tuple-element.42), channel_id=1, source_target_pairs={{0,12},{1,13},{2,14},{3,15},{4,0},{5,1},{6,2},{7,3},{8,4},{9,5},{1... | collective-permute-start | bytes 135176 | tf_op jit(solution)/shard_map/ppermute | solution.py:37
  141.7 2.4 %collective-permute-done.32 = s16[16,1408]{1,0:T(8,128)(2,1)S(1)} collective-permute-done((s16[16,1408]{1,0:T(8,128)(2,1)S(1)}, s16[16,1408]{1,0:T(8,128)(2,1)S(1)}, u32[]{:S(2)}, u32[]{:S(2)}) %collective-permute-start.32) | collective-permute-done | bytes 45088 | tf_op jit(solution)/shard_map/ppermute | solution.py:37
  (138 shorter events, 53.2 us)
Async XLA Ops:
  0.8 18.9 %collective-permute-start.14 = (bf16[80,512]{1,0:T(8,128)(2,1)S(1)}, bf16[80,512]{1,0:T(8,128)(2,1)S(1)}, u32[]{:S(2)}, u32[]{:S(2)}) collective-permute-start(bf16[80,512]{1,0:T(8,128)(2,1)S(1)} %get-tuple-element.62), channel_id=1, source_target_pairs={{0,12},{1,13},{2,14},{3,15},{4,0},{5,1},{6,2},{7,3},{8,4},{9,5},{1... | collective-permute-start | bytes 245768 | tf_op jit(solution)/shard_map/ppermute | solution.py:37
  7.2 12.5 %collective-permute-start.13 = (bf16[80,512]{1,0:T(8,128)(2,1)S(1)}, bf16[80,512]{1,0:T(8,128)(2,1)S(1)}, u32[]{:S(2)}, u32[]{:S(2)}) collective-permute-start(bf16[80,512]{1,0:T(8,128)(2,1)S(1)} %get-tuple-element.62), channel_id=1, source_target_pairs={{0,8},{1,9},{2,10},{3,11},{4,12},{5,13},{6,14},{7,15},{8,0},{9,1},... | collective-permute-start | bytes 245768 | tf_op jit(solution)/shard_map/ppermute | solution.py:37
  8.2 11.5 %collective-permute-start.12 = (bf16[80,512]{1,0:T(8,128)(2,1)S(1)}, bf16[80,512]{1,0:T(8,128)(2,1)S(1)}, u32[]{:S(2)}, u32[]{:S(2)}) collective-permute-start(bf16[80,512]{1,0:T(8,128)(2,1)S(1)} %get-tuple-element.62), channel_id=1, source_target_pairs={{0,4},{1,5},{2,6},{3,7},{4,8},{5,9},{6,10},{7,11},{8,12},{9,13},{1... | collective-permute-start | bytes 245768 | tf_op jit(solution)/shard_map/ppermute | solution.py:37
  14.0 10.9 %collective-permute-start = (s16[16,1408]{1,0:T(8,128)(2,1)S(1)}, s16[16,1408]{1,0:T(8,128)(2,1)S(1)}, u32[]{:S(2)}, u32[]{:S(2)}) collective-permute-start(s16[16,1408]{1,0:T(8,128)(2,1)S(1)} %pad_add_fusion.4), channel_id=1, source_target_pairs={{0,128},{1,144},{2,160},{3,176},{4,192},{5,208},{6,224},{7,240},{8... | collective-permute-start | bytes 135176 | tf_op jit(solution)/shard_map/ppermute | solution.py:37
  19.9 10.6 %collective-permute-start.17 = (bf16[4,80,512]{2,1,0:T(8,128)(2,1)S(1)}, bf16[4,80,512]{2,1,0:T(8,128)(2,1)S(1)}, u32[]{:S(2)}, u32[]{:S(2)}) collective-permute-start(bf16[4,80,512]{2,1,0:T(8,128)(2,1)S(1)} %get-tuple-element.36), channel_id=1, source_target_pairs={{0,3},{1,0},{2,1},{3,2},{4,7},{5,4},{6,5},{7,6},{8,11},{9,8},{10,9... | collective-permute-start | bytes 983048 | tf_op jit(solution)/shard_map/ppermute | solution.py:37
  21.7 12.1 %collective-permute-start.16 = (bf16[4,80,512]{2,1,0:T(8,128)(2,1)S(1)}, bf16[4,80,512]{2,1,0:T(8,128)(2,1)S(1)}, u32[]{:S(2)}, u32[]{:S(2)}) collective-permute-start(bf16[4,80,512]{2,1,0:T(8,128)(2,1)S(1)} %get-tuple-element.36), channel_id=1, source_target_pairs={{0,2},{1,3},{2,0},{3,1},{4,6},{5,7},{6,4},{7,5},{8,10},{9,11},{10,... | collective-permute-start | bytes 983048 | tf_op jit(solution)/shard_map/ppermute | solution.py:37
  23.5 17.1 %collective-permute-start.15 = (bf16[4,80,512]{2,1,0:T(8,128)(2,1)S(1)}, bf16[4,80,512]{2,1,0:T(8,128)(2,1)S(1)}, u32[]{:S(2)}, u32[]{:S(2)}) collective-permute-start(bf16[4,80,512]{2,1,0:T(8,128)(2,1)S(1)} %get-tuple-element.36), channel_id=1, source_target_pairs={{0,1},{1,2},{2,3},{3,0},{4,5},{5,6},{6,7},{7,4},{8,9},{9,10},{10,1... | collective-permute-start | bytes 983048 | tf_op jit(solution)/shard_map/ppermute | solution.py:37
  24.9 16.7 %collective-permute-start.1 = (s16[16,1408]{1,0:T(8,128)(2,1)S(1)}, s16[16,1408]{1,0:T(8,128)(2,1)S(1)}, u32[]{:S(2)}, u32[]{:S(2)}) collective-permute-start(s16[16,1408]{1,0:T(8,128)(2,1)S(1)} %collective-permute-done), channel_id=1, source_target_pairs={{0,32},{1,33},{2,34},{3,35},{4,36},{5,37},{6,38},{7,39},{8,40},{9,... | collective-permute-start | bytes 135176 | tf_op jit(solution)/shard_map/ppermute | solution.py:37
  41.6 10.0 %collective-permute-start.4 = (s16[2,16,1408]{2,1,0:T(8,128)(2,1)S(1)}, s16[2,16,1408]{2,1,0:T(8,128)(2,1)S(1)}, u32[]{:S(2)}, u32[]{:S(2)}) collective-permute-start(s16[2,16,1408]{2,1,0:T(8,128)(2,1)S(1)} %get-tuple-element.57), channel_id=1, source_target_pairs={{0,192},{1,193},{2,194},{3,195},{4,196},{5,197},{6,198},{7,199},{8... | collective-permute-start | bytes 270344 | tf_op jit(solution)/shard_map/ppermute | solution.py:37
  41.7 11.9 %collective-permute-start.3 = (s16[2,16,1408]{2,1,0:T(8,128)(2,1)S(1)}, s16[2,16,1408]{2,1,0:T(8,128)(2,1)S(1)}, u32[]{:S(2)}, u32[]{:S(2)}) collective-permute-start(s16[2,16,1408]{2,1,0:T(8,128)(2,1)S(1)} %get-tuple-element.57), channel_id=1, source_target_pairs={{0,128},{1,129},{2,130},{3,131},{4,132},{5,133},{6,134},{7,135},{8... | collective-permute-start | bytes 270344 | tf_op jit(solution)/shard_map/ppermute | solution.py:37
  42.5 11.1 %collective-permute-start.2 = (s16[2,16,1408]{2,1,0:T(8,128)(2,1)S(1)}, s16[2,16,1408]{2,1,0:T(8,128)(2,1)S(1)}, u32[]{:S(2)}, u32[]{:S(2)}) collective-permute-start(s16[2,16,1408]{2,1,0:T(8,128)(2,1)S(1)} %get-tuple-element.57), channel_id=1, source_target_pairs={{0,64},{1,65},{2,66},{3,67},{4,68},{5,69},{6,70},{7,71},{8,72},{9,... | collective-permute-start | bytes 270344 | tf_op jit(solution)/shard_map/ppermute | solution.py:37
  62.7 9.0 %collective-permute-start.8 = (s16[4,16,1408]{2,1,0:T(8,128)(2,1)S(1)}, s16[4,16,1408]{2,1,0:T(8,128)(2,1)S(1)}, u32[]{:S(2)}, u32[]{:S(2)}) collective-permute-start(s16[4,16,1408]{2,1,0:T(8,128)(2,1)S(1)} %get-tuple-element.16), channel_id=1, source_target_pairs={{0,2},{1,3},{2,0},{3,1},{4,6},{5,7},{6,4},{7,5},{8,10},{9,11},{10,... | collective-permute-start | bytes 540680 | tf_op jit(solution)/shard_map/ppermute | solution.py:37
  64.1 8.0 %collective-permute-start.7 = (s16[4,16,1408]{2,1,0:T(8,128)(2,1)S(1)}, s16[4,16,1408]{2,1,0:T(8,128)(2,1)S(1)}, u32[]{:S(2)}, u32[]{:S(2)}) collective-permute-start(s16[4,16,1408]{2,1,0:T(8,128)(2,1)S(1)} %get-tuple-element.15), channel_id=1, source_target_pairs={{0,3},{1,0},{2,1},{3,2},{4,7},{5,4},{6,5},{7,6},{8,11},{9,8},{10,9... | collective-permute-start | bytes 540680 | tf_op jit(solution)/shard_map/ppermute | solution.py:37
  65.2 8.9 %collective-permute-start.6 = (s16[4,16,1408]{2,1,0:T(8,128)(2,1)S(1)}, s16[4,16,1408]{2,1,0:T(8,128)(2,1)S(1)}, u32[]{:S(2)}, u32[]{:S(2)}) collective-permute-start(s16[4,16,1408]{2,1,0:T(8,128)(2,1)S(1)} %get-tuple-element.14), channel_id=1, source_target_pairs={{0,1},{1,2},{2,3},{3,0},{4,5},{5,6},{6,7},{7,4},{8,9},{9,10},{10,1... | collective-permute-start | bytes 540680 | tf_op jit(solution)/shard_map/ppermute | solution.py:37
  74.8 8.6 %collective-permute-start.11 = (s16[16,1408]{1,0:T(8,128)(2,1)S(1)}, s16[16,1408]{1,0:T(8,128)(2,1)S(1)}, u32[]{:S(2)}, u32[]{:S(2)}) collective-permute-start(s16[16,1408]{1,0:T(8,128)(2,1)S(1)} %get-tuple-element.46), channel_id=1, source_target_pairs={{0,8},{1,9},{2,10},{3,11},{4,12},{5,13},{6,14},{7,15},{8,0},{9,1},... | collective-permute-start | bytes 135176 | tf_op jit(solution)/shard_map/ppermute | solution.py:37
  76.7 6.8 %collective-permute-start.10 = (s16[16,1408]{1,0:T(8,128)(2,1)S(1)}, s16[16,1408]{1,0:T(8,128)(2,1)S(1)}, u32[]{:S(2)}, u32[]{:S(2)}) collective-permute-start(s16[16,1408]{1,0:T(8,128)(2,1)S(1)} %get-tuple-element.45), channel_id=1, source_target_pairs={{0,12},{1,13},{2,14},{3,15},{4,0},{5,1},{6,2},{7,3},{8,4},{9,5},{1... | collective-permute-start | bytes 135176 | tf_op jit(solution)/shard_map/ppermute | solution.py:37
  79.8 6.3 %collective-permute-start.9 = (s16[16,1408]{1,0:T(8,128)(2,1)S(1)}, s16[16,1408]{1,0:T(8,128)(2,1)S(1)}, u32[]{:S(2)}, u32[]{:S(2)}) collective-permute-start(s16[16,1408]{1,0:T(8,128)(2,1)S(1)} %get-tuple-element.44), channel_id=1, source_target_pairs={{0,4},{1,5},{2,6},{3,7},{4,8},{5,9},{6,10},{7,11},{8,12},{9,13},{1... | collective-permute-start | bytes 135176 | tf_op jit(solution)/shard_map/ppermute | solution.py:37
  87.2 9.7 %collective-permute-start.23 = (s16[16,1408]{1,0:T(8,128)(2,1)S(1)}, s16[16,1408]{1,0:T(8,128)(2,1)S(1)}, u32[]{:S(2)}, u32[]{:S(2)}) collective-permute-start(s16[16,1408]{1,0:T(8,128)(2,1)S(1)} %pad_add_fusion.5), channel_id=1, source_target_pairs={{0,128},{1,144},{2,160},{3,176},{4,192},{5,208},{6,224},{7,240},{8... | collective-permute-start | bytes 135176 | tf_op jit(solution)/shard_map/ppermute | solution.py:37
  92.0 7.8 %collective-permute-start.39 = (f32[16,256]{1,0:T(8,128)S(1)}, f32[16,256]{1,0:T(8,128)S(1)}, u32[]{:S(2)}, u32[]{:S(2)}) collective-permute-start(f32[16,256]{1,0:T(8,128)S(1)} %add.264), channel_id=1, source_target_pairs={{0,128},{1,129},{2,130},{3,131},{4,132},{5,133},{6,134},{7,135},{8... | collective-permute-start | bytes 49160 | tf_op jit(solution)/shard_map/ppermute | solution.py:37
  118.1 9.0 %collective-permute-start.31 = (s16[4,16,1408]{2,1,0:T(8,128)(2,1)S(1)}, s16[4,16,1408]{2,1,0:T(8,128)(2,1)S(1)}, u32[]{:S(2)}, u32[]{:S(2)}) collective-permute-start(s16[4,16,1408]{2,1,0:T(8,128)(2,1)S(1)} %get-tuple-element.20), channel_id=1, source_target_pairs={{0,2},{1,3},{2,0},{3,1},{4,6},{5,7},{6,4},{7,5},{8,10},{9,11},{10,... | collective-permute-start | bytes 540680 | tf_op jit(solution)/shard_map/ppermute | solution.py:37
  121.5 9.1 %collective-permute-start.30 = (s16[4,16,1408]{2,1,0:T(8,128)(2,1)S(1)}, s16[4,16,1408]{2,1,0:T(8,128)(2,1)S(1)}, u32[]{:S(2)}, u32[]{:S(2)}) collective-permute-start(s16[4,16,1408]{2,1,0:T(8,128)(2,1)S(1)} %get-tuple-element.19), channel_id=1, source_target_pairs={{0,3},{1,0},{2,1},{3,2},{4,7},{5,4},{6,5},{7,6},{8,11},{9,8},{10,9... | collective-permute-start | bytes 540680 | tf_op jit(solution)/shard_map/ppermute | solution.py:37
  122.4 8.3 %collective-permute-start.29 = (s16[4,16,1408]{2,1,0:T(8,128)(2,1)S(1)}, s16[4,16,1408]{2,1,0:T(8,128)(2,1)S(1)}, u32[]{:S(2)}, u32[]{:S(2)}) collective-permute-start(s16[4,16,1408]{2,1,0:T(8,128)(2,1)S(1)} %get-tuple-element.18), channel_id=1, source_target_pairs={{0,1},{1,2},{2,3},{3,0},{4,5},{5,6},{6,7},{7,4},{8,9},{9,10},{10,1... | collective-permute-start | bytes 540680 | tf_op jit(solution)/shard_map/ppermute | solution.py:37
  131.3 8.6 %collective-permute-start.34 = (s16[16,1408]{1,0:T(8,128)(2,1)S(1)}, s16[16,1408]{1,0:T(8,128)(2,1)S(1)}, u32[]{:S(2)}, u32[]{:S(2)}) collective-permute-start(s16[16,1408]{1,0:T(8,128)(2,1)S(1)} %get-tuple-element.43), channel_id=1, source_target_pairs={{0,8},{1,9},{2,10},{3,11},{4,12},{5,13},{6,14},{7,15},{8,0},{9,1},... | collective-permute-start | bytes 135176 | tf_op jit(solution)/shard_map/ppermute | solution.py:37
  135.3 6.3 %collective-permute-start.33 = (s16[16,1408]{1,0:T(8,128)(2,1)S(1)}, s16[16,1408]{1,0:T(8,128)(2,1)S(1)}, u32[]{:S(2)}, u32[]{:S(2)}) collective-permute-start(s16[16,1408]{1,0:T(8,128)(2,1)S(1)} %get-tuple-element.42), channel_id=1, source_target_pairs={{0,12},{1,13},{2,14},{3,15},{4,0},{5,1},{6,2},{7,3},{8,4},{9,5},{1... | collective-permute-start | bytes 135176 | tf_op jit(solution)/shard_map/ppermute | solution.py:37
  (17 other events, 88.7 us)
where the time goes:
time: 147 us; the launch traced here: 145 us
  starting transfers between devices  65 us (44%)
  waiting for transfers between devices  54 us (37%)
  Pallas kernels  13.4 us (9%)
  other arithmetic  8.02 us (5%)
  local copies, waits for them, and re-layouts  2.2 us (1%)
  matrix products  2.06 us (1%)
    ppermute x40, starting transfers between devices, send(): return lax.ppermute(value, AXES, pairs)  65 us
    ppermute x40, waiting for transfers between devices, send(): return lax.ppermute(value, AXES, pairs)  54 us
    pallas_call x2, Pallas kernels, respond(): pl.pallas_call(respond_body, in_specs=[smem, vmem, vmem, pl.BlockSpec(mem...  13.4 us
  transfers between devices with their start and end apart: 40, of which 22 were waited for; matrix products, arithmetic and copies ran while one was open for 6% of the time, Pallas kernels for 0%

commit v1 on v0

--- a/solution.py
+++ b/solution.py
@@ -92,7 +92,7 @@
     return lax.dot_general(left, right, ((contract[0], contract[1]), ((), ())), preferred_element_type=jnp.float32)
 
 
-def respond_body(place_ref, own_core_ref, other_core_ref, prior_ref, own_ref, *refs):
+def respond_body(place_ref, own_core_ref, other_core_ref, gain_ref, prior_ref, own_ref, *refs):
     sent, (rows_ref, sum_ref, kept_ref, sems) = refs[:3], refs[3:]
     copies = []
     for at in range(1280 // BLOCK):
@@ -105,7 +105,7 @@
             for d in range(2):
                 coded = ref[s, d]
                 power = coded[:, 1280:].astype(jnp.float32)[:, :1]
-                value = coded[:, :1280].astype(jnp.float32) * (jnp.exp2(power) * (1.0 / FULL))
+                value = coded[:, :1280].astype(jnp.float32) * (jnp.exp2(power) * (1.0 / FULL)) * gain_ref[...]
                 high = value.astype(jnp.bfloat16)
                 low = (value - high.astype(jnp.float32)).astype(jnp.bfloat16)
                 block = ((along_y - s + 2) & 3) * 4 + ((near_z + d) & 1) * 2 + ((core + k) & 1)
@@ -135,11 +135,11 @@
             sent[step - 1][z, :, 1280:] = powers.astype(jnp.int16)
 
 
-def respond(own_core, other_core, prior, place):
+def respond(own_core, other_core, gain, prior, place):
     smem, vmem = pl.BlockSpec(memory_space=pltpu.SMEM), pl.BlockSpec(memory_space=pltpu.VMEM)
     return pl.pallas_call(
         respond_body,
-        in_specs=[smem, vmem, vmem, pl.BlockSpec(memory_space=pltpu.HBM)],
+        in_specs=[smem, vmem, vmem, vmem, pl.BlockSpec(memory_space=pltpu.HBM)],
         out_specs=[vmem] * 4,
         out_shape=[jax.ShapeDtypeStruct((4, 16, 1280), jnp.float32)]
         + [jax.ShapeDtypeStruct((4, 16, 1408), jnp.int16)] * 3,
@@ -152,7 +152,28 @@
         compiler_params=pltpu.CompilerParams(vmem_limit_bytes=48 << 20),
         cost_estimate=pl.CostEstimate(flops=3400000000, transcendentals=0, bytes_accessed=8000000),
         name="respond",
-    )(place, own_core, other_core, prior)
+    )(place, own_core, other_core, gain, prior)
+
+
+def prepare_body(value_ref, coded_ref):
+    value = value_ref[...]
+    top = jnp.max(jnp.abs(value), axis=-1, keepdims=True)
+    power = jnp.clip(jnp.ceil(jnp.log2(jnp.maximum(top, 1e-30))), -100.0, 125.0)
+    scaled = jnp.round(value * (jnp.exp2(-power) * FULL)).astype(jnp.int32)
+    coded_ref[:, :1280] = scaled.astype(jnp.int16)
+    coded_ref[:, 1280:] = jnp.broadcast_to(power.astype(jnp.int32), (16, 128)).astype(jnp.int16)
+
+
+def prepare(value):
+    vmem = pl.BlockSpec(memory_space=pltpu.VMEM)
+    return pl.pallas_call(
+        prepare_body,
+        in_specs=[vmem],
+        out_specs=vmem,
+        out_shape=jax.ShapeDtypeStruct((16, 1408), jnp.int16),
+        compiler_params=pltpu.CompilerParams(vmem_limit_bytes=8 << 20),
+        name="prepare",
+    )(value)
 
 
 def project(scaled, weighted):
@@ -191,13 +212,14 @@
     block = jnp.concatenate([pairs[0].T, pairs[1].T], axis=1)
     iterate = potential
     for step in range(ITERS):
-        coded = send(encode(iterate * gain), SWAP)
+        coded = send(encode(iterate) if step else prepare(iterate), SWAP)
         if step == 0:
             elements = gather_cols(block, col_index).reshape(1280, 512)
             weights = 1.0 / (pick_energy(cond_band, cond_energy) - pick_energy(val_band, val_energy))
             weights = jnp.concatenate([weights, weights])
+            gain_col = lax.dynamic_slice_in_dim(coul_root, col_index * 1280, 1280, 0).reshape(1, 1280)
             weighted = (weights[None, :] * elements.astype(jnp.float32)).astype(jnp.bfloat16)
-        own, *sent = respond(*gather_rows(coded), prior, place)
+        own, *sent = respond(*gather_rows(coded), gain_col, prior, place)
         reduced = reduce_cols(own, sent, col_index >> 2)
         projected = project(iterate * gain, weighted)
         projected = sum_rows(projected) / NG

time: 147 us -> 147 us (level)
    pallas_call x2 -> x3, Pallas kernels: 13.4 us -> 13.6 us  [the longest x2 13.4 us: respond(): pl.pallas_call(respond_body, in_specs=[smem, vmem, vmem, vmem, pl.BlockSp...]
  transfers between devices with their start and end apart: 40 -> 40, of which waited for: 22 -> 22; matrix products, arithmetic and copies ran while one was open for 6% -> 5% of each run, Pallas kernels for 0% -> 0%
where the time goes in v1:
time: 147 us; the launch traced here: 145 us
  starting transfers between devices  64.6 us (44%)
  waiting for transfers between devices  54.5 us (37%)
  Pallas kernels  13.6 us (9%)
  other arithmetic  6.92 us (5%)
  local copies, waits for them, and re-layouts  2.87 us (2%)
  matrix products  2.07 us (1%)
    ppermute x40, starting transfers between devices, send(): return lax.ppermute(value, AXES, pairs)  64.6 us
    ppermute x40, waiting for transfers between devices, send(): return lax.ppermute(value, AXES, pairs)  54.5 us
    pallas_call x2, Pallas kernels, respond(): pl.pallas_call(respond_body, in_specs=[smem, vmem, vmem, vmem, pl.BlockSp...  13.4 us
  transfers between devices with their start and end apart: 40, of which 22 were waited for; matrix products, arithmetic and copies ran while one was open for 5% of the time, Pallas kernels for 0%

profile of v1, /device:TPU:8, one launch (start us, length us, event | category | flops | bytes accessed | tf_op | source)
XLA Modules:
  0.0 145.0 jit_solution(2632003318074434448)
XLA Ops:
  0.8 6.4 %collective-permute-start.14 = (bf16[80,512]{1,0:T(8,128)(2,1)S(1)}, bf16[80,512]{1,0:T(8,128)(2,1)S(1)}, u32[]{:S(2)}, u32[]{:S(2)}) collective-permute-start(bf16[80,512]{1,0:T(8,128)(2,1)S(1)} %get-tuple-element.63), channel_id=1, source_target_pairs={{0,12},{1,13},{2,14},{3,15},{4,0},{5,1},{6,2},{7,3},{8,4},{9,5},{1... | collective-permute-start | bytes 245768 | tf_op jit(solution)/shard_map/ppermute | solution.py:37
  8.2 2.8 %collective-permute-start.12 = (bf16[80,512]{1,0:T(8,128)(2,1)S(1)}, bf16[80,512]{1,0:T(8,128)(2,1)S(1)}, u32[]{:S(2)}, u32[]{:S(2)}) collective-permute-start(bf16[80,512]{1,0:T(8,128)(2,1)S(1)} %get-tuple-element.63), channel_id=1, source_target_pairs={{0,4},{1,5},{2,6},{3,7},{4,8},{5,9},{6,10},{7,11},{8,12},{9,13},{1... | collective-permute-start | bytes 245768 | tf_op jit(solution)/shard_map/ppermute | solution.py:37
  12.0 3.8 %collective-permute-start = (s16[16,1408]{1,0:T(8,128)(2,1)S(1)}, s16[16,1408]{1,0:T(8,128)(2,1)S(1)}, u32[]{:S(2)}, u32[]{:S(2)}) collective-permute-start(s16[16,1408]{1,0:T(8,128)(2,1)S(1)} %prepare.1), channel_id=1, source_target_pairs={{0,128},{1,144},{2,160},{3,176},{4,192},{5,208},{6,224},{7,240},{8... | collective-permute-start | bytes 135176 | tf_op jit(solution)/shard_map/ppermute | solution.py:37
  25.4 4.9 %collective-permute-done.17 = bf16[4,80,512]{2,1,0:T(8,128)(2,1)S(1)} collective-permute-done((bf16[4,80,512]{2,1,0:T(8,128)(2,1)S(1)}, bf16[4,80,512]{2,1,0:T(8,128)(2,1)S(1)}, u32[]{:S(2)}, u32[]{:S(2)}) %collective-permute-start.17) | collective-permute-done | bytes 327712 | tf_op jit(solution)/shard_map/ppermute | solution.py:37
  30.2 3.4 %collective-permute-done.16 = bf16[4,80,512]{2,1,0:T(8,128)(2,1)S(1)} collective-permute-done((bf16[4,80,512]{2,1,0:T(8,128)(2,1)S(1)}, bf16[4,80,512]{2,1,0:T(8,128)(2,1)S(1)}, u32[]{:S(2)}, u32[]{:S(2)}) %collective-permute-start.16) | collective-permute-done | bytes 327712 | tf_op jit(solution)/shard_map/ppermute | solution.py:37
  33.7 6.7 %collective-permute-done.15 = bf16[4,80,512]{2,1,0:T(8,128)(2,1)S(1)} collective-permute-done((bf16[4,80,512]{2,1,0:T(8,128)(2,1)S(1)}, bf16[4,80,512]{2,1,0:T(8,128)(2,1)S(1)}, u32[]{:S(2)}, u32[]{:S(2)}) %collective-permute-start.15) | collective-permute-done | bytes 327712 | tf_op jit(solution)/shard_map/ppermute | solution.py:37
  47.5 3.9 %collective-permute-start.22 = (f32[16,256]{1,0:T(8,128)S(1)}, f32[16,256]{1,0:T(8,128)S(1)}, u32[]{:S(2)}, u32[]{:S(2)}) collective-permute-start(f32[16,256]{1,0:T(8,128)S(1)} %add.250), channel_id=1, source_target_pairs={{0,128},{1,129},{2,130},{3,131},{4,132},{5,133},{6,134},{7,135},{8... | collective-permute-start | bytes 49160 | tf_op jit(solution)/shard_map/ppermute | solution.py:37
  51.4 2.0 %collective-permute-start.21 = (f32[16,256]{1,0:T(8,128)S(1)}, f32[16,256]{1,0:T(8,128)S(1)}, u32[]{:S(2)}, u32[]{:S(2)}) collective-permute-start(f32[16,256]{1,0:T(8,128)S(1)} %add.250), channel_id=1, source_target_pairs={{0,192},{1,193},{2,194},{3,195},{4,196},{5,197},{6,198},{7,199},{8... | collective-permute-start | bytes 49160 | tf_op jit(solution)/shard_map/ppermute | solution.py:37
  55.8 6.7 %respond.2 = (f32[4,16,1280]{2,1,0:T(8,128)S(1)}, s16[4,16,1408]{2,1,0:T(8,128)(2,1)S(1)}, s16[4,16,1408]{2,1,0:T(8,128)(2,1)S(1)}, s16[4,16,1408]{2,1,0:T(8,128)(2,1)S(1)}) custom-call(s32[4]{0:T(128)S(1)} %pad_add_fusion.5.place_ref, s16[4,2,16,1408]{3,2,1,0:T(8,128)(2,1)S(1)} %pad_add_fusion.own_core_ref, ...), custom_call_target="tpu_custom_call" | custom-call | flops 3400000000 | bytes 8000000 | tf_op jit(solution)/shard_map/respond/pallas_call | solution.py:140
  66.0 5.6 %collective-permute-done.8 = s16[4,16,1408]{2,1,0:T(8,128)(2,1)S(1)} collective-permute-done((s16[4,16,1408]{2,1,0:T(8,128)(2,1)S(1)}, s16[4,16,1408]{2,1,0:T(8,128)(2,1)S(1)}, u32[]{:S(2)}, u32[]{:S(2)}) %collective-permute-start.8) | collective-permute-done | bytes 180256 | tf_op jit(solution)/shard_map/ppermute | solution.py:37
  72.0 2.0 %collective-permute-done.6 = s16[4,16,1408]{2,1,0:T(8,128)(2,1)S(1)} collective-permute-done((s16[4,16,1408]{2,1,0:T(8,128)(2,1)S(1)}, s16[4,16,1408]{2,1,0:T(8,128)(2,1)S(1)}, u32[]{:S(2)}, u32[]{:S(2)}) %collective-permute-start.6) | collective-permute-done | bytes 180256 | tf_op jit(solution)/shard_map/ppermute | solution.py:37
  76.6 3.1 %collective-permute-start.10 = (s16[16,1408]{1,0:T(8,128)(2,1)S(1)}, s16[16,1408]{1,0:T(8,128)(2,1)S(1)}, u32[]{:S(2)}, u32[]{:S(2)}) collective-permute-start(s16[16,1408]{1,0:T(8,128)(2,1)S(1)} %get-tuple-element.45), channel_id=1, source_target_pairs={{0,12},{1,13},{2,14},{3,15},{4,0},{5,1},{6,2},{7,3},{8,4},{9,5},{1... | collective-permute-start | bytes 135176 | tf_op jit(solution)/shard_map/ppermute | solution.py:37
  79.7 3.5 %collective-permute-done.11 = s16[16,1408]{1,0:T(8,128)(2,1)S(1)} collective-permute-done((s16[16,1408]{1,0:T(8,128)(2,1)S(1)}, s16[16,1408]{1,0:T(8,128)(2,1)S(1)}, u32[]{:S(2)}, u32[]{:S(2)}) %collective-permute-start.11) | collective-permute-done | bytes 45088 | tf_op jit(solution)/shard_map/ppermute | solution.py:37
  83.4 2.5 %collective-permute-done.9 = s16[16,1408]{1,0:T(8,128)(2,1)S(1)} collective-permute-done((s16[16,1408]{1,0:T(8,128)(2,1)S(1)}, s16[16,1408]{1,0:T(8,128)(2,1)S(1)}, u32[]{:S(2)}, u32[]{:S(2)}) %collective-permute-start.9) | collective-permute-done | bytes 45088 | tf_op jit(solution)/shard_map/ppermute | solution.py:37
  89.8 2.0 %collective-permute-done.36 = f32[16,256]{1,0:T(8,128)S(1)} collective-permute-done((f32[16,256]{1,0:T(8,128)S(1)}, f32[16,256]{1,0:T(8,128)S(1)}, u32[]{:S(2)}, u32[]{:S(2)}) %collective-permute-start.36) | collective-permute-done | bytes 16416 | tf_op jit(solution)/shard_map/ppermute | solution.py:37
  96.0 4.1 %collective-permute-start.24 = (s16[16,1408]{1,0:T(8,128)(2,1)S(1)}, s16[16,1408]{1,0:T(8,128)(2,1)S(1)}, u32[]{:S(2)}, u32[]{:S(2)}) collective-permute-start(s16[16,1408]{1,0:T(8,128)(2,1)S(1)} %collective-permute-done.23), channel_id=1, source_target_pairs={{0,32},{1,33},{2,34},{3,35},{4,36},{5,37},{6,38},{7,39},{8,40},{9,... | collective-permute-start | bytes 135176 | tf_op jit(solution)/shard_map/ppermute | solution.py:37
  103.6 2.5 %collective-permute-start.25 = (s16[2,16,1408]{2,1,0:T(8,128)(2,1)S(1)}, s16[2,16,1408]{2,1,0:T(8,128)(2,1)S(1)}, u32[]{:S(2)}, u32[]{:S(2)}) collective-permute-start(s16[2,16,1408]{2,1,0:T(8,128)(2,1)S(1)} %get-tuple-element.52), channel_id=1, source_target_pairs={{0,64},{1,65},{2,66},{3,67},{4,68},{5,69},{6,70},{7,71},{8,72},{9,... | collective-permute-start | bytes 270344 | tf_op jit(solution)/shard_map/ppermute | solution.py:37
  111.6 6.7 %respond.3 = (f32[4,16,1280]{2,1,0:T(8,128)S(1)}, s16[4,16,1408]{2,1,0:T(8,128)(2,1)S(1)}, s16[4,16,1408]{2,1,0:T(8,128)(2,1)S(1)}, s16[4,16,1408]{2,1,0:T(8,128)(2,1)S(1)}) custom-call(s32[4]{0:T(128)S(1)} %pad_add_fusion.5.place_ref, s16[4,2,16,1408]{3,2,1,0:T(8,128)(2,1)S(1)} %pad_add_fusion.1.own_core_ref, ...), custom_call_target="tpu_custom_call" | custom-call | flops 3400000000 | bytes 8000000 | tf_op jit(solution)/shard_map/respond/pallas_call | solution.py:140
  118.3 3.1 %collective-permute-start.31 = (s16[4,16,1408]{2,1,0:T(8,128)(2,1)S(1)}, s16[4,16,1408]{2,1,0:T(8,128)(2,1)S(1)}, u32[]{:S(2)}, u32[]{:S(2)}) collective-permute-start(s16[4,16,1408]{2,1,0:T(8,128)(2,1)S(1)} %get-tuple-element.20), channel_id=1, source_target_pairs={{0,2},{1,3},{2,0},{3,1},{4,6},{5,7},{6,4},{7,5},{8,10},{9,11},{10,... | collective-permute-start | bytes 540680 | tf_op jit(solution)/shard_map/ppermute | solution.py:37
  123.5 3.8 %collective-permute-done.31 = s16[4,16,1408]{2,1,0:T(8,128)(2,1)S(1)} collective-permute-done((s16[4,16,1408]{2,1,0:T(8,128)(2,1)S(1)}, s16[4,16,1408]{2,1,0:T(8,128)(2,1)S(1)}, u32[]{:S(2)}, u32[]{:S(2)}) %collective-permute-start.31) | collective-permute-done | bytes 180256 | tf_op jit(solution)/shard_map/ppermute | solution.py:37
  127.4 3.1 %collective-permute-done.30 = s16[4,16,1408]{2,1,0:T(8,128)(2,1)S(1)} collective-permute-done((s16[4,16,1408]{2,1,0:T(8,128)(2,1)S(1)}, s16[4,16,1408]{2,1,0:T(8,128)(2,1)S(1)}, u32[]{:S(2)}, u32[]{:S(2)}) %collective-permute-start.30) | collective-permute-done | bytes 180256 | tf_op jit(solution)/shard_map/ppermute | solution.py:37
  131.2 4.0 %collective-permute-start.34 = (s16[16,1408]{1,0:T(8,128)(2,1)S(1)}, s16[16,1408]{1,0:T(8,128)(2,1)S(1)}, u32[]{:S(2)}, u32[]{:S(2)}) collective-permute-start(s16[16,1408]{1,0:T(8,128)(2,1)S(1)} %get-tuple-element.43), channel_id=1, source_target_pairs={{0,8},{1,9},{2,10},{3,11},{4,12},{5,13},{6,14},{7,15},{8,0},{9,1},... | collective-permute-start | bytes 135176 | tf_op jit(solution)/shard_map/ppermute | solution.py:37
  135.3 2.7 %collective-permute-start.33 = (s16[16,1408]{1,0:T(8,128)(2,1)S(1)}, s16[16,1408]{1,0:T(8,128)(2,1)S(1)}, u32[]{:S(2)}, u32[]{:S(2)}) collective-permute-start(s16[16,1408]{1,0:T(8,128)(2,1)S(1)} %get-tuple-element.42), channel_id=1, source_target_pairs={{0,12},{1,13},{2,14},{3,15},{4,0},{5,1},{6,2},{7,3},{8,4},{9,5},{1... | collective-permute-start | bytes 135176 | tf_op jit(solution)/shard_map/ppermute | solution.py:37
  141.4 2.7 %collective-permute-done.32 = s16[16,1408]{1,0:T(8,128)(2,1)S(1)} collective-permute-done((s16[16,1408]{1,0:T(8,128)(2,1)S(1)}, s16[16,1408]{1,0:T(8,128)(2,1)S(1)}, u32[]{:S(2)}, u32[]{:S(2)}) %collective-permute-start.32) | collective-permute-done | bytes 45088 | tf_op jit(solution)/shard_map/ppermute | solution.py:37
  (136 shorter events, 52.5 us)
Async XLA Ops:
  0.8 18.6 %collective-permute-start.14 = (bf16[80,512]{1,0:T(8,128)(2,1)S(1)}, bf16[80,512]{1,0:T(8,128)(2,1)S(1)}, u32[]{:S(2)}, u32[]{:S(2)}) collective-permute-start(bf16[80,512]{1,0:T(8,128)(2,1)S(1)} %get-tuple-element.63), channel_id=1, source_target_pairs={{0,12},{1,13},{2,14},{3,15},{4,0},{5,1},{6,2},{7,3},{8,4},{9,5},{1... | collective-permute-start | bytes 245768 | tf_op jit(solution)/shard_map/ppermute | solution.py:37
  7.2 12.3 %collective-permute-start.13 = (bf16[80,512]{1,0:T(8,128)(2,1)S(1)}, bf16[80,512]{1,0:T(8,128)(2,1)S(1)}, u32[]{:S(2)}, u32[]{:S(2)}) collective-permute-start(bf16[80,512]{1,0:T(8,128)(2,1)S(1)} %get-tuple-element.63), channel_id=1, source_target_pairs={{0,8},{1,9},{2,10},{3,11},{4,12},{5,13},{6,14},{7,15},{8,0},{9,1},... | collective-permute-start | bytes 245768 | tf_op jit(solution)/shard_map/ppermute | solution.py:37
  8.2 11.3 %collective-permute-start.12 = (bf16[80,512]{1,0:T(8,128)(2,1)S(1)}, bf16[80,512]{1,0:T(8,128)(2,1)S(1)}, u32[]{:S(2)}, u32[]{:S(2)}) collective-permute-start(bf16[80,512]{1,0:T(8,128)(2,1)S(1)} %get-tuple-element.63), channel_id=1, source_target_pairs={{0,4},{1,5},{2,6},{3,7},{4,8},{5,9},{6,10},{7,11},{8,12},{9,13},{1... | collective-permute-start | bytes 245768 | tf_op jit(solution)/shard_map/ppermute | solution.py:37
  12.0 12.7 %collective-permute-start = (s16[16,1408]{1,0:T(8,128)(2,1)S(1)}, s16[16,1408]{1,0:T(8,128)(2,1)S(1)}, u32[]{:S(2)}, u32[]{:S(2)}) collective-permute-start(s16[16,1408]{1,0:T(8,128)(2,1)S(1)} %prepare.1), channel_id=1, source_target_pairs={{0,128},{1,144},{2,160},{3,176},{4,192},{5,208},{6,224},{7,240},{8... | collective-permute-start | bytes 135176 | tf_op jit(solution)/shard_map/ppermute | solution.py:37
  19.7 10.6 %collective-permute-start.17 = (bf16[4,80,512]{2,1,0:T(8,128)(2,1)S(1)}, bf16[4,80,512]{2,1,0:T(8,128)(2,1)S(1)}, u32[]{:S(2)}, u32[]{:S(2)}) collective-permute-start(bf16[4,80,512]{2,1,0:T(8,128)(2,1)S(1)} %get-tuple-element.36), channel_id=1, source_target_pairs={{0,3},{1,0},{2,1},{3,2},{4,7},{5,4},{6,5},{7,6},{8,11},{9,8},{10,9... | collective-permute-start | bytes 983048 | tf_op jit(solution)/shard_map/ppermute | solution.py:37
  21.5 12.1 %collective-permute-start.16 = (bf16[4,80,512]{2,1,0:T(8,128)(2,1)S(1)}, bf16[4,80,512]{2,1,0:T(8,128)(2,1)S(1)}, u32[]{:S(2)}, u32[]{:S(2)}) collective-permute-start(bf16[4,80,512]{2,1,0:T(8,128)(2,1)S(1)} %get-tuple-element.36), channel_id=1, source_target_pairs={{0,2},{1,3},{2,0},{3,1},{4,6},{5,7},{6,4},{7,5},{8,10},{9,11},{10,... | collective-permute-start | bytes 983048 | tf_op jit(solution)/shard_map/ppermute | solution.py:37
  23.3 17.1 %collective-permute-start.15 = (bf16[4,80,512]{2,1,0:T(8,128)(2,1)S(1)}, bf16[4,80,512]{2,1,0:T(8,128)(2,1)S(1)}, u32[]{:S(2)}, u32[]{:S(2)}) collective-permute-start(bf16[4,80,512]{2,1,0:T(8,128)(2,1)S(1)} %get-tuple-element.36), channel_id=1, source_target_pairs={{0,1},{1,2},{2,3},{3,0},{4,5},{5,6},{6,7},{7,4},{8,9},{9,10},{10,1... | collective-permute-start | bytes 983048 | tf_op jit(solution)/shard_map/ppermute | solution.py:37
  24.7 16.7 %collective-permute-start.1 = (s16[16,1408]{1,0:T(8,128)(2,1)S(1)}, s16[16,1408]{1,0:T(8,128)(2,1)S(1)}, u32[]{:S(2)}, u32[]{:S(2)}) collective-permute-start(s16[16,1408]{1,0:T(8,128)(2,1)S(1)} %collective-permute-done), channel_id=1, source_target_pairs={{0,32},{1,33},{2,34},{3,35},{4,36},{5,37},{6,38},{7,39},{8,40},{9,... | collective-permute-start | bytes 135176 | tf_op jit(solution)/shard_map/ppermute | solution.py:37
  41.4 10.0 %collective-permute-start.4 = (s16[2,16,1408]{2,1,0:T(8,128)(2,1)S(1)}, s16[2,16,1408]{2,1,0:T(8,128)(2,1)S(1)}, u32[]{:S(2)}, u32[]{:S(2)}) collective-permute-start(s16[2,16,1408]{2,1,0:T(8,128)(2,1)S(1)} %get-tuple-element.56), channel_id=1, source_target_pairs={{0,192},{1,193},{2,194},{3,195},{4,196},{5,197},{6,198},{7,199},{8... | collective-permute-start | bytes 270344 | tf_op jit(solution)/shard_map/ppermute | solution.py:37
  41.5 11.9 %collective-permute-start.3 = (s16[2,16,1408]{2,1,0:T(8,128)(2,1)S(1)}, s16[2,16,1408]{2,1,0:T(8,128)(2,1)S(1)}, u32[]{:S(2)}, u32[]{:S(2)}) collective-permute-start(s16[2,16,1408]{2,1,0:T(8,128)(2,1)S(1)} %get-tuple-element.56), channel_id=1, source_target_pairs={{0,128},{1,129},{2,130},{3,131},{4,132},{5,133},{6,134},{7,135},{8... | collective-permute-start | bytes 270344 | tf_op jit(solution)/shard_map/ppermute | solution.py:37
  42.3 11.1 %collective-permute-start.2 = (s16[2,16,1408]{2,1,0:T(8,128)(2,1)S(1)}, s16[2,16,1408]{2,1,0:T(8,128)(2,1)S(1)}, u32[]{:S(2)}, u32[]{:S(2)}) collective-permute-start(s16[2,16,1408]{2,1,0:T(8,128)(2,1)S(1)} %get-tuple-element.56), channel_id=1, source_target_pairs={{0,64},{1,65},{2,66},{3,67},{4,68},{5,69},{6,70},{7,71},{8,72},{9,... | collective-permute-start | bytes 270344 | tf_op jit(solution)/shard_map/ppermute | solution.py:37
  62.6 9.0 %collective-permute-start.8 = (s16[4,16,1408]{2,1,0:T(8,128)(2,1)S(1)}, s16[4,16,1408]{2,1,0:T(8,128)(2,1)S(1)}, u32[]{:S(2)}, u32[]{:S(2)}) collective-permute-start(s16[4,16,1408]{2,1,0:T(8,128)(2,1)S(1)} %get-tuple-element.16), channel_id=1, source_target_pairs={{0,2},{1,3},{2,0},{3,1},{4,6},{5,7},{6,4},{7,5},{8,10},{9,11},{10,... | collective-permute-start | bytes 540680 | tf_op jit(solution)/shard_map/ppermute | solution.py:37
  63.9 8.0 %collective-permute-start.7 = (s16[4,16,1408]{2,1,0:T(8,128)(2,1)S(1)}, s16[4,16,1408]{2,1,0:T(8,128)(2,1)S(1)}, u32[]{:S(2)}, u32[]{:S(2)}) collective-permute-start(s16[4,16,1408]{2,1,0:T(8,128)(2,1)S(1)} %get-tuple-element.15), channel_id=1, source_target_pairs={{0,3},{1,0},{2,1},{3,2},{4,7},{5,4},{6,5},{7,6},{8,11},{9,8},{10,9... | collective-permute-start | bytes 540680 | tf_op jit(solution)/shard_map/ppermute | solution.py:37
  65.1 8.9 %collective-permute-start.6 = (s16[4,16,1408]{2,1,0:T(8,128)(2,1)S(1)}, s16[4,16,1408]{2,1,0:T(8,128)(2,1)S(1)}, u32[]{:S(2)}, u32[]{:S(2)}) collective-permute-start(s16[4,16,1408]{2,1,0:T(8,128)(2,1)S(1)} %get-tuple-element.14), channel_id=1, source_target_pairs={{0,1},{1,2},{2,3},{3,0},{4,5},{5,6},{6,7},{7,4},{8,9},{9,10},{10,1... | collective-permute-start | bytes 540680 | tf_op jit(solution)/shard_map/ppermute | solution.py:37
  74.6 8.6 %collective-permute-start.11 = (s16[16,1408]{1,0:T(8,128)(2,1)S(1)}, s16[16,1408]{1,0:T(8,128)(2,1)S(1)}, u32[]{:S(2)}, u32[]{:S(2)}) collective-permute-start(s16[16,1408]{1,0:T(8,128)(2,1)S(1)} %get-tuple-element.46), channel_id=1, source_target_pairs={{0,8},{1,9},{2,10},{3,11},{4,12},{5,13},{6,14},{7,15},{8,0},{9,1},... | collective-permute-start | bytes 135176 | tf_op jit(solution)/shard_map/ppermute | solution.py:37
  76.6 6.7 %collective-permute-start.10 = (s16[16,1408]{1,0:T(8,128)(2,1)S(1)}, s16[16,1408]{1,0:T(8,128)(2,1)S(1)}, u32[]{:S(2)}, u32[]{:S(2)}) collective-permute-start(s16[16,1408]{1,0:T(8,128)(2,1)S(1)} %get-tuple-element.45), channel_id=1, source_target_pairs={{0,12},{1,13},{2,14},{3,15},{4,0},{5,1},{6,2},{7,3},{8,4},{9,5},{1... | collective-permute-start | bytes 135176 | tf_op jit(solution)/shard_map/ppermute | solution.py:37
  79.7 6.3 %collective-permute-start.9 = (s16[16,1408]{1,0:T(8,128)(2,1)S(1)}, s16[16,1408]{1,0:T(8,128)(2,1)S(1)}, u32[]{:S(2)}, u32[]{:S(2)}) collective-permute-start(s16[16,1408]{1,0:T(8,128)(2,1)S(1)} %get-tuple-element.44), channel_id=1, source_target_pairs={{0,4},{1,5},{2,6},{3,7},{4,8},{5,9},{6,10},{7,11},{8,12},{9,13},{1... | collective-permute-start | bytes 135176 | tf_op jit(solution)/shard_map/ppermute | solution.py:37
  87.0 9.0 %collective-permute-start.23 = (s16[16,1408]{1,0:T(8,128)(2,1)S(1)}, s16[16,1408]{1,0:T(8,128)(2,1)S(1)}, u32[]{:S(2)}, u32[]{:S(2)}) collective-permute-start(s16[16,1408]{1,0:T(8,128)(2,1)S(1)} %pad_add_fusion.4), channel_id=1, source_target_pairs={{0,128},{1,144},{2,160},{3,176},{4,192},{5,208},{6,224},{7,240},{8... | collective-permute-start | bytes 135176 | tf_op jit(solution)/shard_map/ppermute | solution.py:37
  91.9 8.2 %collective-permute-start.39 = (f32[16,256]{1,0:T(8,128)S(1)}, f32[16,256]{1,0:T(8,128)S(1)}, u32[]{:S(2)}, u32[]{:S(2)}) collective-permute-start(f32[16,256]{1,0:T(8,128)S(1)} %add.268), channel_id=1, source_target_pairs={{0,128},{1,129},{2,130},{3,131},{4,132},{5,133},{6,134},{7,135},{8... | collective-permute-start | bytes 49160 | tf_op jit(solution)/shard_map/ppermute | solution.py:37
  93.4 6.7 %collective-permute-start.37 = (f32[16,256]{1,0:T(8,128)S(1)}, f32[16,256]{1,0:T(8,128)S(1)}, u32[]{:S(2)}, u32[]{:S(2)}) collective-permute-start(f32[16,256]{1,0:T(8,128)S(1)} %add.268), channel_id=1, source_target_pairs={{0,64},{1,65},{2,66},{3,67},{4,68},{5,69},{6,70},{7,71},{8,72},{9,... | collective-permute-start | bytes 49160 | tf_op jit(solution)/shard_map/ppermute | solution.py:37
  118.3 9.0 %collective-permute-start.31 = (s16[4,16,1408]{2,1,0:T(8,128)(2,1)S(1)}, s16[4,16,1408]{2,1,0:T(8,128)(2,1)S(1)}, u32[]{:S(2)}, u32[]{:S(2)}) collective-permute-start(s16[4,16,1408]{2,1,0:T(8,128)(2,1)S(1)} %get-tuple-element.20), channel_id=1, source_target_pairs={{0,2},{1,3},{2,0},{3,1},{4,6},{5,7},{6,4},{7,5},{8,10},{9,11},{10,... | collective-permute-start | bytes 540680 | tf_op jit(solution)/shard_map/ppermute | solution.py:37
  121.4 9.1 %collective-permute-start.30 = (s16[4,16,1408]{2,1,0:T(8,128)(2,1)S(1)}, s16[4,16,1408]{2,1,0:T(8,128)(2,1)S(1)}, u32[]{:S(2)}, u32[]{:S(2)}) collective-permute-start(s16[4,16,1408]{2,1,0:T(8,128)(2,1)S(1)} %get-tuple-element.19), channel_id=1, source_target_pairs={{0,3},{1,0},{2,1},{3,2},{4,7},{5,4},{6,5},{7,6},{8,11},{9,8},{10,9... | collective-permute-start | bytes 540680 | tf_op jit(solution)/shard_map/ppermute | solution.py:37
  122.3 8.3 %collective-permute-start.29 = (s16[4,16,1408]{2,1,0:T(8,128)(2,1)S(1)}, s16[4,16,1408]{2,1,0:T(8,128)(2,1)S(1)}, u32[]{:S(2)}, u32[]{:S(2)}) collective-permute-start(s16[4,16,1408]{2,1,0:T(8,128)(2,1)S(1)} %get-tuple-element.18), channel_id=1, source_target_pairs={{0,1},{1,2},{2,3},{3,0},{4,5},{5,6},{6,7},{7,4},{8,9},{9,10},{10,1... | collective-permute-start | bytes 540680 | tf_op jit(solution)/shard_map/ppermute | solution.py:37
  131.2 8.6 %collective-permute-start.34 = (s16[16,1408]{1,0:T(8,128)(2,1)S(1)}, s16[16,1408]{1,0:T(8,128)(2,1)S(1)}, u32[]{:S(2)}, u32[]{:S(2)}) collective-permute-start(s16[16,1408]{1,0:T(8,128)(2,1)S(1)} %get-tuple-element.43), channel_id=1, source_target_pairs={{0,8},{1,9},{2,10},{3,11},{4,12},{5,13},{6,14},{7,15},{8,0},{9,1},... | collective-permute-start | bytes 135176 | tf_op jit(solution)/shard_map/ppermute | solution.py:37
  (18 other events, 93.1 us)
